TPU v7x, 32 devices: a whole 2x2x4 slice. The times are simulated.
32 devices in a mesh: cond: 4 (over y, x), shard: 8 (over z, core).
Axes of the slice: x: 2, y: 2, z: 4, core: 2. Of those that a mesh axis runs over, the one named last changes fastest.
Arguments:
- expression: bfloat16 [2048, 2048], P(('cond', 'shard')), may hold values from -6 to 6
- responses: bfloat16 [2048, 512], P(('cond', 'shard')), may hold values from -200 to 200
- coef_init: float32 [8192, 512], P(('cond', 'shard')), may hold values from -4 to 4
- dual_init: float32 [8192, 512], P(('cond', 'shard')), may hold values from -3 to 3
- penalty: float32 [2048], P('shard'), may hold values from 0.5 to 4
Outputs:
- coefficients: float32 [8192, 512], P(('cond', 'shard'))
- consensus: float32 [8192, 512], P(('cond', 'shard'))
- duals: float32 [8192, 512], P(('cond', 'shard'))
All inputs are finite; a program needn't handle non-finite values.
Results may differ from a plain program's by a relative error of at most 0.0045.
Values may be sent and summed in bfloat16 or wider, within the bound.
No kernel may reach another device: no remote copies, remote signals or barrier semaphores. Data moves between devices by JAX's collectives and lax.ppermute only.
A program may use at most 64 MiB of HBM per device.

v0:
```python
import jax
import jax.numpy as jnp
from jax import lax
from jax.sharding import PartitionSpec as P

ITERS = 2
rho_weight = 2.0


def shards(expression, responses, coef_init, dual_init, penalty):
    my_rows = coef_init.shape[0]
    row_start = lax.axis_index("shard") * my_rows
    n_cells = expression.shape[0] * lax.axis_size("shard")
    contract = (((0,), (0,)), ((), ()))
    piece_x = lax.all_gather(expression, "shard", axis=0, tiled=True)
    piece_y = lax.all_gather(responses, "shard", axis=0, tiled=True)
    owned = lax.dynamic_slice_in_dim(piece_x, row_start, my_rows, 1)
    gram = lax.dot_general(owned, piece_x, contract, preferred_element_type=jnp.float32)
    cross = lax.dot_general(owned, piece_y, contract, preferred_element_type=jnp.float32)
    gram, cross = (gram, cross)
    gram = gram / n_cells
    cross = cross / n_cells
    diagonal = jnp.diagonal(lax.dynamic_slice_in_dim(gram, row_start, my_rows, 1))
    gram_copy = gram.astype(jnp.bfloat16)
    coef = coef_init
    dual = dual_init
    weights = penalty[:, None]
    consensus = coef
    for step in range(ITERS):
        merged = coef + dual
        norms = jnp.sqrt(lax.psum(merged * merged, "cond"))
        consensus = merged * (1.0 - weights / jnp.maximum(norms, weights))
        dual = merged - consensus
        coef_copy = coef.astype(jnp.bfloat16)
        product = jnp.dot(
            gram_copy,
            lax.all_gather(coef_copy, "shard", axis=0, tiled=True),
            preferred_element_type=jnp.float32,
        )
        coef = coef + (cross + rho_weight * (consensus - dual) - product - rho_weight * coef) / (
            diagonal[:, None] + rho_weight
        )
    return (coef, consensus, dual)


def solution(mesh):
    in_specs = (
        P(("cond", "shard"), None),
        P(("cond", "shard"), None),
        P(("cond", "shard"), None),
        P(("cond", "shard"), None),
        P("shard"),
    )
    out_specs = (P(("cond", "shard"), None), P(("cond", "shard"), None), P(("cond", "shard"), None))
    return jax.shard_map(shards, mesh=mesh, in_specs=in_specs, out_specs=out_specs, check_vma=False)
```

profile of v0, /device:TPU:0, one launch (start us, length us, event | category | flops | bytes accessed | tf_op | source)
XLA Modules:
  0.0 136.4 jit_solution(8652733695643158765)
XLA Ops:
  8.0 0.0 copy-start.1
  8.0 0.0 all-gather.4.cloned.1.call-start
  8.1 0.7 all-gather.4.cloned.1.call-update
  8.7 0.0 all-reduce.3.cloned.1.call-start
  8.8 2.5 %fusion.17 = (f32[256,512]{1,0:T(8,128)}, f32[256,512]{1,0:T(8,128)}, bf16[256,512]{1,0:T(8,128)(2,1)}) fusion(f32[256,512]{1,0:T(8,128)} %param.7, f32[256,512]{1,0:T(8,128)} %param.8), kind=kLoop, calls=%fused_computation.26 | loop fusion | flops 393216 | bytes 2359296 | tf_op jit(solution)/shard_map/mul | solution.py:31
  11.3 0.0 all-reduce.3.cloned.1.call-update
  11.3 0.0 all-gather.6.cloned.1.call-start
  11.4 0.7 all-gather.6.cloned.1.call-update
  12.1 0.0 all-reduce.5.cloned.1.call-start
  12.2 0.0 copy-done.1
  12.2 17.8 %all_gather.13 = bf16[512,512]{1,0:T(8,128)(2,1)S(1)} all-gather(bf16[64,512]{1,0:T(8,128)(2,1)S(1)} %copy-done.1), channel_id=1, replica_groups=mesh['cond'=4,'shard'=8] {'shard'}, dimensions={0}, use_global_device_ids=true | all-gather | bytes 589824 | tf_op jit(solution)/shard_map/all_gather | solution.py:16
  29.9 13.9 %all-gather.4.cloned.1.call-done = bf16[512,2048]{1,0:T(8,128)(2,1)} async-done(((bf16[64,2048]{1,0:T(8,128)(2,1)}), bf16[512,2048]{1,0:T(8,128)(2,1)}) %all-gather.4.cloned.1.call-update) | async-done | bytes 2097168 | tf_op jit(solution)/shard_map/all_gather | solution.py:15
  43.9 2.4 %convolution_multiply_fusion = f32[256,2048]{1,0:T(8,128)S(1)} fusion(bf16[512,2048]{1,0:T(8,128)(2,1)} %all-gather.4.cloned.1.call-done, s32[]{:T(128)S(6)} %select_n.8), kind=kOutput, calls=%fused_computation.1 | convolution fusion | flops 537395200 | bytes 4456452 | tf_op jit(solution)/shard_map/dot_general | solution.py:18
  46.3 0.0 copy-start.2
  46.3 2.3 %gather_fusion = f32[256]{0:T(256)S(1)} fusion(f32[256,256]{1,0:T(8,128)S(1)} %constant_dynamic-slice_fusion, s32[256]{0:T(256)S(1)} %bitcast.5), kind=kCustom, calls=%fused_computation | custom fusion | bytes 4096 | tf_op jit(solution)/shard_map/jit(diagonal)/cond/branch_0_fun/gather | solution.py:23
  48.7 1.3 convolution_multiply_fusion.1
  50.0 10.3 %all-reduce.3.cloned.1.call-done = f32[256,512]{1,0:T(8,128)} async-done(((f32[256,512]{1,0:T(8,128)}), f32[256,512]{1,0:T(8,128)}) %all-reduce.3.cloned.1.call-update) | async-done | bytes 524304 | tf_op jit(solution)/shard_map/psum | solution.py:31
  60.3 14.7 %all-gather.6.cloned.1.call-done = bf16[2048,512]{1,0:T(8,128)(2,1)} async-done(((bf16[256,512]{1,0:T(8,128)(2,1)}), bf16[2048,512]{1,0:T(8,128)(2,1)}) %all-gather.6.cloned.1.call-update) | async-done | bytes 2097168 | tf_op jit(solution)/shard_map/all_gather | solution.py:37
  75.0 0.0 copy-done.2
  75.0 4.2 %fusion.15 = (f32[256,512]{1,0:T(8,128)}, f32[256,512]{1,0:T(8,128)}, bf16[256,512]{1,0:T(8,128)(2,1)}, f32[256,512]{1,0:T(8,128)}) fusion(f32[256,512]{1,0:T(8,128)} %get-tuple-element.8, f32[256,512]{1,0:T(8,128)} %all-reduce.3.cloned.1.call-done, f32[256]{0:T(256)S(1)} %copy-done.2, f32[256,512]{1,0:T(8,128)} %param.7, f32[256]{0:T(256)S(1)} %broadcast_add_fusion, ...), kind=kOutput, calls=%fused_computation.25 | convolution fusion | flops 539492352 | bytes 8128512 | tf_op jit(solution)/shard_map/dot_general | solution.py:35
  79.1 0.0 all-reduce.5.cloned.1.call-update
  79.2 0.0 all-gather.8.cloned.1.call-start
  79.2 0.7 all-gather.8.cloned.1.call-update
  79.9 43.6 %all-reduce.5.cloned.1.call-done = f32[256,512]{1,0:T(8,128)} async-done(((f32[256,512]{1,0:T(8,128)}), f32[256,512]{1,0:T(8,128)}) %all-reduce.5.cloned.1.call-update) | async-done | bytes 524304 | tf_op jit(solution)/shard_map/psum | solution.py:31
  123.5 2.2 %fusion.14 = (f32[256,512]{1,0:T(8,128)S(1)}, f32[256,512]{1,0:T(8,128)}) fusion(f32[256,512]{1,0:T(8,128)} %get-tuple-element.6, f32[256,512]{1,0:T(8,128)} %all-reduce.5.cloned.1.call-done, f32[256]{0:T(256)S(1)} %copy-done.2), kind=kLoop, calls=%fused_computation.24 | loop fusion | flops 655360 | bytes 2098176 | tf_op jit(solution)/shard_map/sub | solution.py:33
  125.8 0.0 copy-start
  125.8 0.0 all-gather.8.cloned.1.call-done
  125.8 3.6 %fusion.4 = f32[256,512]{1,0:T(8,128)} fusion(f32[256,512]{1,0:T(8,128)} %get-tuple-element.11, bf16[2048,512]{1,0:T(8,128)(2,1)} %all-gather.8.cloned.1.call-done, f32[256,512]{1,0:T(8,128)S(1)} %convolution_multiply_fusion.1, f32[256,512]{1,0:T(8,128)} %get-tuple-element.4, f32[256,512]{1,0:T(8,128)S(1)} %get-tuple-element.3, ...), kind=kOutput, calls=%fused_computation.9 | convolution fusion | flops 538443776 | bytes 6816768 | tf_op jit(solution)/shard_map/dot_general | solution.py:35
  129.3 0.0 copy-done
  (3 shorter events, 0.0 us)
Async XLA Ops:
  8.0 4.2 %copy-start.1 = (bf16[64,512]{1,0:T(8,128)(2,1)S(1)}, bf16[64,512]{1,0:T(8,128)(2,1)}, u32[]{:S(2)}) copy-start(bf16[64,512]{1,0:T(8,128)(2,1)} %param.6) | copy-start | bytes 196612
  8.0 35.8 %all-gather.4.cloned.1.call-start = ((), (), s32[]{:S(2)}) async-start(), calls=%async_computation | async-start | bytes 2359296 | tf_op jit(solution)/shard_map/all_gather | solution.py:15
  8.7 51.5 %all-reduce.3.cloned.1.call-start = ((), (), s32[]{:S(2)}) async-start(), calls=%async_computation.1 | async-start | bytes 1048576 | tf_op jit(solution)/shard_map/psum | solution.py:31
  11.3 63.6 %all-gather.6.cloned.1.call-start = ((), (), s32[]{:S(2)}) async-start(), calls=%async_computation.2 | async-start | bytes 2359296 | tf_op jit(solution)/shard_map/all_gather | solution.py:37
  12.1 111.4 %all-reduce.5.cloned.1.call-start = ((), (), s32[]{:S(2)}) async-start(), calls=%async_computation.3 | async-start | bytes 1048576 | tf_op jit(solution)/shard_map/psum | solution.py:31
  46.3 28.7 %copy-start.2 = (f32[256]{0:T(256)S(1)}, f32[256]{0:T(256)}, u32[]{:S(2)}) copy-start(f32[256]{0:T(256)} %param.9) | copy-start | bytes 3076
  79.2 46.6 %all-gather.8.cloned.1.call-start = ((), (), s32[]{:S(2)}) async-start(), calls=%async_computation.4 | async-start | bytes 2359296 | tf_op jit(solution)/shard_map/all_gather | solution.py:37
  125.8 3.6 %copy-start = (f32[256,512]{1,0:T(8,128)}, f32[256,512]{1,0:T(8,128)S(1)}, u32[]{:S(2)}) copy-start(f32[256,512]{1,0:T(8,128)S(1)} %get-tuple-element.3) | copy-start | bytes 1572868
Sparse Core Ops, SparseCore 0:
  10.4 33.3 all-gather.3
  46.0 28.9 all-gather.5
  81.6 28.5 all-gather.7
Sparse Core Ops, SparseCore 1:
  12.8 47.4 all-reduce.2
  79.3 44.2 all-reduce.4
where the time goes:
time: 137 us; the launch traced here: 136 us
  waiting for transfers between devices  84.6 us (62%)
  blocking collectives  17.8 us (13%)
  between operations  15.3 us (11%)
  matrix products  11.4 us (8%)
  other arithmetic  4.75 us (3%)
  local copies, waits for them, and re-layouts  2.38 us (2%)
    psum x2, waiting for transfers between devices, shards(): norms = jnp.sqrt(lax.psum(merged * merged, 'cond'))  53.9 us
    all_gather x1, blocking collectives, shards(): piece_y = lax.all_gather(responses, 'shard', axis=0, tiled=True)  17.8 us
    all_gather x2, waiting for transfers between devices, shards(): lax.all_gather(coef_copy, 'shard', axis=0, tiled=True)  14.7 us
    all_gather x1, waiting for transfers between devices, shards(): piece_x = lax.all_gather(expression, 'shard', axis=0, tiled=True)  13.9 us
    dot_general x2, matrix products, shards(): jnp.dot(gram_copy, lax.all_gather(coef_copy, 'shard', axis=0, tiled=True)...  7.73 us
  transfers between devices with their start and end apart: 5, of which 4 were waited for; matrix products, arithmetic and copies ran while one was open for 8% of the time, Pallas kernels for 0%

commit v1 on v0

--- a/solution.py
+++ b/solution.py
@@ -7,12 +7,24 @@
 rho_weight = 2.0
 
 
+def collect(x, axis, dim):
+    ways, here, hop = (lax.axis_size(axis), lax.axis_index(axis), x.shape[dim])
+    line, have = (x, 1)
+    while have < ways:
+        line = jnp.concatenate(
+            [line, lax.ppermute(line, axis, [(d, (d - have) % ways) for d in range(ways)])],
+            axis=dim,
+        )
+        have = 2 * have
+    return jnp.roll(line, here * hop, axis=dim)
+
+
 def shards(expression, responses, coef_init, dual_init, penalty):
     my_rows = coef_init.shape[0]
     row_start = lax.axis_index("shard") * my_rows
     n_cells = expression.shape[0] * lax.axis_size("shard")
     contract = (((0,), (0,)), ((), ()))
-    piece_x = lax.all_gather(expression, "shard", axis=0, tiled=True)
+    piece_x = collect(expression, "shard", 0)
     piece_y = lax.all_gather(responses, "shard", axis=0, tiled=True)
     owned = lax.dynamic_slice_in_dim(piece_x, row_start, my_rows, 1)
     gram = lax.dot_general(owned, piece_x, contract, preferred_element_type=jnp.float32)

time: 137 us -> 174 us (1.27)
  blocking collectives: 17.8 us -> 68.9 us
  waiting for transfers between devices: 84.6 us -> 60.6 us
  starting transfers between devices: 0.21 us -> 5.33 us
  other arithmetic: 4.75 us -> 9.29 us
  local copies, waits for them, and re-layouts: 2.38 us -> 4.63 us
  matrix products: 11.4 us -> 9.38 us
    all_gather x1, blocking collectives: 17.8 us -> 68.9 us  [shards(): piece_y = lax.all_gather(responses, 'shard', axis=0, tiled=True)]
    ppermute x0 -> x3, waiting for transfers between devices: none -> 16.7 us  [collect(): lax.ppermute(line, axis, [(d, (d - have) % ways) for d in range(ways)])]
    all_gather x2, waiting for transfers between devices: 14.7 us -> 0.03 us  [shards(): lax.all_gather(coef_copy, 'shard', axis=0, tiled=True)]
    all_gather x1 -> x0, waiting for transfers between devices: 13.9 us -> none  [shards(): piece_x = lax.all_gather(expression, 'shard', axis=0, tiled=True)]
    psum x2, waiting for transfers between devices: 53.9 us -> 43.3 us  [shards(): norms = jnp.sqrt(lax.psum(merged * merged, 'cond'))]
    ppermute x0 -> x3, starting transfers between devices: none -> 5.16 us  [collect(): lax.ppermute(line, axis, [(d, (d - have) % ways) for d in range(ways)])]
    mul x1 -> x2, other arithmetic: 2.52 us -> 4.83 us  [shards(): norms = jnp.sqrt(lax.psum(merged * merged, 'cond'))]
    unnamed x6 -> x17, local copies, waits for them, and re-layouts: 0.01 us -> 2.19 us
  transfers between devices with their start and end apart: 5 -> 7, of which waited for: 4 -> 3; matrix products, arithmetic and copies ran while one was open for 8% -> 7% of each run, Pallas kernels for 0% -> 0%
where the time goes in v1:
time: 174 us
  blocking collectives  68.9 us (40%)
  waiting for transfers between devices  60.6 us (35%)
  between operations  15.7 us (9%)
  matrix products  9.38 us (5%)
  other arithmetic  9.29 us (5%)
  starting transfers between devices  5.33 us (3%)
  local copies, waits for them, and re-layouts  4.63 us (3%)
    all_gather x1, blocking collectives, shards(): piece_y = lax.all_gather(responses, 'shard', axis=0, tiled=True)  68.9 us
    psum x2, waiting for transfers between devices, shards(): norms = jnp.sqrt(lax.psum(merged * merged, 'cond'))  43.3 us
    ppermute x3, waiting for transfers between devices, collect(): lax.ppermute(line, axis, [(d, (d - have) % ways) for d in range(ways)])  16.7 us
    dot_general x2, matrix products, shards(): jnp.dot(gram_copy, lax.all_gather(coef_copy, 'shard', axis=0, tiled=True)...  7.06 us
    ppermute x3, starting transfers between devices, collect(): lax.ppermute(line, axis, [(d, (d - have) % ways) for d in range(ways)])  5.16 us
    mul x2, other arithmetic, shards(): norms = jnp.sqrt(lax.psum(merged * merged, 'cond'))  4.83 us
  transfers between devices with their start and end apart: 7, of which 3 were waited for; matrix products, arithmetic and copies ran while one was open for 7% of the time, Pallas kernels for 0%

profile of v1, /device:TPU:0, one launch (start us, length us, event | category | flops | bytes accessed | tf_op | source)
XLA Modules:
  0.0 173.8 jit_solution(11202179526646606164)
XLA Ops:
  8.0 0.0 copy-start
  8.0 0.0 copy-start.3
  8.0 0.0 all-reduce.3.cloned.1.call-start
  8.1 4.5 %collective-permute-start = (bf16[64,2048]{1,0:T(8,128)(2,1)}, bf16[64,2048]{1,0:T(8,128)(2,1)S(1)}, u32[]{:S(2)}, u32[]{:S(2)}) collective-permute-start(bf16[64,2048]{1,0:T(8,128)(2,1)} %param.5), channel_id=1, source_target_pairs={{0,7},{1,0},{2,1},{3,2},{4,3},{5,4},{6,5},{7,6},{8,15},{9,8},{10,9... | collective-permute-start | bytes 786440 | tf_op jit(solution)/shard_map/ppermute | solution.py:15
  12.6 2.5 %fusion.16 = (f32[256,512]{1,0:T(8,128)}, f32[256,512]{1,0:T(8,128)}, bf16[256,512]{1,0:T(8,128)(2,1)}) fusion(f32[256,512]{1,0:T(8,128)} %param.7, f32[256,512]{1,0:T(8,128)} %param.8), kind=kLoop, calls=%fused_computation.33 | loop fusion | flops 393216 | bytes 2359296 | tf_op jit(solution)/shard_map/mul | solution.py:43
  15.2 0.0 all-reduce.3.cloned.1.call-update
  15.2 0.0 all-gather.3.cloned.1.call-start
  15.2 1.6 collective-permute-done
  16.8 1.0 pad_maximum_fusion.1
  17.8 0.6 collective-permute-start.1
  18.4 0.0 all-gather.3.cloned.1.call-update
  18.4 0.0 all-reduce.5.cloned.1.call-start
  18.5 15.1 %collective-permute-done.1 = bf16[128,2048]{1,0:T(8,128)(2,1)S(1)} collective-permute-done((bf16[128,2048]{1,0:T(8,128)(2,1)S(1)}, bf16[128,2048]{1,0:T(8,128)(2,1)S(1)}, u32[]{:S(2)}, u32[]{:S(2)}) %collective-permute-start.1) | collective-permute-done | bytes 524320 | tf_op jit(solution)/shard_map/ppermute | solution.py:15
  33.6 0.0 copy-done
  33.6 1.1 pad_maximum_fusion
  34.7 0.0 collective-permute-start.2
  34.7 0.0 copy-done.3
  34.7 68.9 %all_gather.9 = bf16[512,512]{1,0:T(8,128)(2,1)S(1)} all-gather(bf16[64,512]{1,0:T(8,128)(2,1)S(1)} %copy-done.3), channel_id=1, replica_groups=mesh['cond'=4,'shard'=8] {'shard'}, dimensions={0}, use_global_device_ids=true | all-gather | bytes 589824 | tf_op jit(solution)/shard_map/all_gather | solution.py:28
  103.6 0.0 collective-permute-done.2
  103.6 0.1 constant_dynamic-update-slice_fusion.4
  103.8 0.1 constant_dynamic-update-slice_fusion
  103.9 0.0 copy-start.1
  103.9 1.9 %copy-done.1 = bf16[1024,2048]{1,0:T(8,128)(2,1)} copy-done((bf16[1024,2048]{1,0:T(8,128)(2,1)}, bf16[1024,2048]{1,0:T(8,128)(2,1)S(1)}, u32[]{:S(2)}) %copy-start.1) | copy-done | bytes 4194328
  105.9 0.0 copy-start.4
  105.9 0.8 convolution_multiply_fusion
  106.7 2.3 %gather_fusion = f32[256]{0:T(256)S(1)} fusion(f32[256,256]{1,0:T(8,128)S(1)} %constant_dynamic-slice_fusion, s32[256]{0:T(256)S(1)} %bitcast.4), kind=kCustom, calls=%fused_computation | custom fusion | bytes 4096 | tf_op jit(solution)/shard_map/jit(diagonal)/cond/branch_0_fun/gather | solution.py:35
  109.1 1.5 convolution_multiply_fusion.1
  110.6 0.0 all-reduce.3.cloned.1.call-done
  110.6 0.0 all-gather.3.cloned.1.call-done
  110.6 0.0 copy-start.2
  110.7 0.0 copy-done.4
  110.7 3.7 %fusion.12 = (bf16[256,512]{1,0:T(8,128)(2,1)}, f32[256,512]{1,0:T(8,128)S(1)}) fusion(f32[256,512]{1,0:T(8,128)} %param.7, f32[256]{0:T(256)S(1)} %broadcast_add_fusion, f32[256,512]{1,0:T(8,128)S(1)} %convolution_multiply_fusion.1, f32[256,512]{1,0:T(8,128)} %get-tuple-element.10, f32[256,512]{1,0:T(8,128)} %all-reduce.3.cloned.1.call-done, ...), kind=kOutput, calls=%fused_computation.30 | convolution fusion | flops 539230208 | bytes 7079936 | tf_op jit(solution)/shard_map/dot_general | solution.py:47
  114.4 0.0 copy-done.2
  114.4 2.3 %fusion.14 = (f32[256,512]{1,0:T(8,128)}, f32[256,512]{1,0:T(8,128)}) fusion(f32[256,512]{1,0:T(8,128)S(1)} %get-tuple-element.4, f32[256,512]{1,0:T(8,128)} %get-tuple-element.10, f32[256,512]{1,0:T(8,128)S(1)} %copy-done.2, f32[256]{0:T(256)S(1)} %copy-done.4), kind=kLoop, calls=%fused_computation.32 | loop fusion | flops 917504 | bytes 2622464 | tf_op jit(solution)/shard_map/mul | solution.py:43
  116.6 0.0 all-reduce.5.cloned.1.call-update
  116.7 0.0 all-gather.5.cloned.1.call-start
  116.7 0.5 all-gather.5.cloned.1.call-update
  117.3 43.3 %all-reduce.5.cloned.1.call-done = f32[256,512]{1,0:T(8,128)} async-done(((f32[256,512]{1,0:T(8,128)}), f32[256,512]{1,0:T(8,128)}) %all-reduce.5.cloned.1.call-update) | async-done | bytes 524304 | tf_op jit(solution)/shard_map/psum | solution.py:43
  160.6 2.4 %fusion.13 = (f32[256,512]{1,0:T(8,128)}, f32[256,512]{1,0:T(8,128)}) fusion(f32[256,512]{1,0:T(8,128)} %get-tuple-element.8, f32[256,512]{1,0:T(8,128)} %all-reduce.5.cloned.1.call-done, f32[256]{0:T(256)S(1)} %copy-done.4), kind=kLoop, calls=%fused_computation.31 | loop fusion | flops 655360 | bytes 2098176 | tf_op jit(solution)/shard_map/sub | solution.py:45
  163.0 0.0 all-gather.5.cloned.1.call-done
  163.0 3.4 %divide_add_fusion = f32[256,512]{1,0:T(8,128)} fusion(f32[256,512]{1,0:T(8,128)S(1)} %get-tuple-element.4, f32[256,512]{1,0:T(8,128)S(1)} %convolution_multiply_fusion.1, f32[256,512]{1,0:T(8,128)} %get-tuple-element.6, f32[256,512]{1,0:T(8,128)} %get-tuple-element.5, bf16[2048,512]{1,0:T(8,128)(2,1)} %all-gather.5.cloned.1.call-done, ...), kind=kOutput, calls=%fused_computation.6 | convolution fusion | flops 538443776 | bytes 6816768 | tf_op jit(solution)/shard_map/dot_general | solution.py:47
  (9 shorter events, 0.2 us)
Async XLA Ops:
  8.0 25.6 %copy-start = (bf16[64,2048]{1,0:T(8,128)(2,1)S(1)}, bf16[64,2048]{1,0:T(8,128)(2,1)}, u32[]{:S(2)}) copy-start(bf16[64,2048]{1,0:T(8,128)(2,1)} %param.5) | copy-start | bytes 786436
  8.0 26.7 %copy-start.3 = (bf16[64,512]{1,0:T(8,128)(2,1)S(1)}, bf16[64,512]{1,0:T(8,128)(2,1)}, u32[]{:S(2)}) copy-start(bf16[64,512]{1,0:T(8,128)(2,1)} %param.6) | copy-start | bytes 196612
  8.0 102.6 %all-reduce.3.cloned.1.call-start = ((), (), s32[]{:S(2)}) async-start(), calls=%async_computation | async-start | bytes 1048576 | tf_op jit(solution)/shard_map/psum | solution.py:43
  8.1 8.7 %collective-permute-start = (bf16[64,2048]{1,0:T(8,128)(2,1)}, bf16[64,2048]{1,0:T(8,128)(2,1)S(1)}, u32[]{:S(2)}, u32[]{:S(2)}) collective-permute-start(bf16[64,2048]{1,0:T(8,128)(2,1)} %param.5), channel_id=1, source_target_pairs={{0,7},{1,0},{2,1},{3,2},{4,3},{5,4},{6,5},{7,6},{8,15},{9,8},{10,9... | collective-permute-start | bytes 786440 | tf_op jit(solution)/shard_map/ppermute | solution.py:15
  15.2 95.5 %all-gather.3.cloned.1.call-start = ((), (), s32[]{:S(2)}) async-start(), calls=%async_computation.1 | async-start | bytes 2359296 | tf_op jit(solution)/shard_map/all_gather | solution.py:49
  17.8 15.8 %collective-permute-start.1 = (bf16[128,2048]{1,0:T(8,128)(2,1)S(1)}, bf16[128,2048]{1,0:T(8,128)(2,1)S(1)}, u32[]{:S(2)}, u32[]{:S(2)}) collective-permute-start(bf16[128,2048]{1,0:T(8,128)(2,1)S(1)} %pad_maximum_fusion.1), channel_id=1, source_target_pairs={{0,6},{1,7},{2,0},{3,1},{4,2},{5,3},{6,4},{7,5},{8,14},{9,15},{10,... | collective-permute-start | bytes 1572872 | tf_op jit(solution)/shard_map/ppermute | solution.py:15
  18.4 142.1 %all-reduce.5.cloned.1.call-start = ((), (), s32[]{:S(2)}) async-start(), calls=%async_computation.2 | async-start | bytes 1048576 | tf_op jit(solution)/shard_map/psum | solution.py:43
  34.7 69.0 %collective-permute-start.2 = (bf16[256,2048]{1,0:T(8,128)(2,1)}, bf16[256,2048]{1,0:T(8,128)(2,1)S(1)}, u32[]{:S(2)}, u32[]{:S(2)}) collective-permute-start(bf16[256,2048]{1,0:T(8,128)(2,1)} %pad_maximum_fusion), channel_id=1, source_target_pairs={{0,4},{1,5},{2,6},{3,7},{4,0},{5,1},{6,2},{7,3},{8,12},{9,13},{10,... | collective-permute-start | bytes 3145736 | tf_op jit(solution)/shard_map/ppermute | solution.py:15
  103.9 2.0 %copy-start.1 = (bf16[1024,2048]{1,0:T(8,128)(2,1)}, bf16[1024,2048]{1,0:T(8,128)(2,1)S(1)}, u32[]{:S(2)}) copy-start(bf16[1024,2048]{1,0:T(8,128)(2,1)S(1)} %constant_dynamic-update-slice_fusion) | copy-start | bytes 12582916
  105.9 4.8 %copy-start.4 = (f32[256]{0:T(256)S(1)}, f32[256]{0:T(256)}, u32[]{:S(2)}) copy-start(f32[256]{0:T(256)} %param.9) | copy-start | bytes 3076
  110.6 3.7 %copy-start.2 = (f32[256,512]{1,0:T(8,128)S(1)}, f32[256,512]{1,0:T(8,128)}, u32[]{:S(2)}) copy-start(f32[256,512]{1,0:T(8,128)} %all-reduce.3.cloned.1.call-done) | copy-start | bytes 1572868
  116.7 46.3 %all-gather.5.cloned.1.call-start = ((), (), s32[]{:S(2)}) async-start(), calls=%async_computation.3 | async-start | bytes 2359296 | tf_op jit(solution)/shard_map/all_gather | solution.py:49
Sparse Core Ops, SparseCore 0:
  15.3 45.1 all-reduce.2
  116.8 43.7 all-reduce.4
Sparse Core Ops, SparseCore 1:
  18.5 57.8 all-gather.2
  118.7 27.4 all-gather.4
